TPU v7x, 32 devices: a whole 2x2x4 slice. The times are simulated.
32 devices in a mesh: groups: 2 (over y), seq: 4 (over z), blk: 2 (over x), hd: 2 (over core).
Axes of the slice: x: 2, y: 2, z: 4, core: 2. Of those that a mesh axis runs over, the one named last changes fastest.
Arguments:
- query_raw: bfloat16 [8192, 2048], P(('groups', 'seq', 'blk'), 'hd'), parts along dimension 0, may hold values from -6 to 6
- key_raw: bfloat16 [8192, 2048], P(('groups', 'seq', 'blk'), 'hd'), parts along dimension 0, may hold values from -6 to 6
- value_raw: bfloat16 [8192, 2048], P(('groups', 'seq', 'blk'), 'hd'), parts along dimension 0, may hold values from -6 to 6
- beta_rate: float32 [8192, 16], P(('groups', 'seq', 'blk'), 'hd'), parts along dimension 0, may hold values from 0 to 1
- conv_weight: float32 [3, 4, 2048], P(None, None, 'hd'), may hold values from -3 to 3
- out_gain: float32 [128], replicated, may hold values from 0.1 to 1.9
Outputs:
- head_output: bfloat16 [8192, 2048], P(('groups', 'seq', 'blk'), 'hd'), parts along dimension 0
There are 2 independent parts, one for each index of `groups`. A program takes and returns all parts, laid end to end along the dimension named above; an argument that names none is the same for every part. Nothing has to cross between parts.
All inputs are finite; a program needn't handle non-finite values.
Results may differ from a plain program's by a relative error of at most 0.0064.
Values may be sent and summed in bfloat16 or wider, within the bound.
A program may use at most 192 MiB of HBM per device.

v0:
```python
import jax
import jax.numpy as jnp
from jax import lax
from jax.sharding import PartitionSpec as P

SPAN = 64


PRECISE = lax.Precision.HIGHEST


def shifted(array, axis, by):
    devices = lax.axis_size(axis)
    pairs = [(i, i + by) for i in range(devices) if 0 <= i + by < devices]
    return lax.ppermute(array, axis, pairs)


def prefix(array, axis, combine, identity):
    devices, index = (lax.axis_size(axis), lax.axis_index(axis))
    everything = jax.tree.map(lambda part: lax.all_gather(part, axis), array)
    start = jax.tree.map(
        lambda part, zero: jnp.broadcast_to(jnp.asarray(zero, part.dtype), part.shape),
        array,
        identity,
    )

    def lap(k, before):
        reached = k < index
        new = combine(before, jax.tree.map(lambda part: part[k], everything))
        return jax.tree.map(lambda a, b: jnp.where(reached, a, b), new, before)

    return lax.fori_loop(0, devices, lap, start)


def short_conv(raw, earlier, weights):
    kernel_len = weights.shape[0]
    tok_rows = raw.shape[0]
    padded = jnp.concatenate((earlier, raw), axis=0).astype(jnp.float32)
    summed = jnp.zeros(raw.shape, jnp.float32)
    for offset in range(kernel_len):
        summed = summed + weights[offset] * padded[offset : offset + tok_rows]
    return jax.nn.silu(summed)


def compose(earlier, later):
    early_map, early_add = earlier
    late_map, late_add = later
    joined_map = jnp.einsum("hde,hef->hdf", late_map, early_map, precision=PRECISE)
    joined_add = jnp.einsum("hde,hef->hdf", late_map, early_add, precision=PRECISE) + late_add
    return (joined_map, joined_add)


def unit_lower_inverse(lower_part, span_len):
    power = -lower_part
    inverse = jnp.eye(span_len, dtype=jnp.float32) + power
    factor_count = (span_len - 1).bit_length()
    for level in range(1, factor_count):
        power = jnp.einsum("nhcs,nhst->nhct", power, power, precision=PRECISE)
        inverse = inverse + jnp.einsum("nhcs,nhst->nhct", inverse, power, precision=PRECISE)
    return inverse


def on_device(query_raw, key_raw, value_raw, beta_rate, conv_weight, out_gain):
    tok_rows = query_raw.shape[0]
    head_count = beta_rate.shape[1]
    key_dim = query_raw.shape[1] // head_count
    value_dim = value_raw.shape[1] // head_count
    rim_rows = conv_weight.shape[1] - 1
    rim_stack = jnp.stack(
        (
            query_raw[tok_rows - rim_rows :],
            key_raw[tok_rows - rim_rows :],
            value_raw[tok_rows - rim_rows :],
        )
    )
    before = shifted(rim_stack, ("seq", "blk"), 1)
    queries = short_conv(query_raw, before[0], conv_weight[0]).astype(jnp.bfloat16)
    conv_k = short_conv(key_raw, before[1], conv_weight[1]).reshape(tok_rows, head_count, key_dim)
    keys_norm = (
        conv_k * lax.rsqrt(jnp.sum(conv_k * conv_k, axis=-1, keepdims=True) + 1e-06)
    ).astype(jnp.bfloat16)
    values = short_conv(value_raw, before[2], conv_weight[2]).astype(jnp.bfloat16)
    span_count = tok_rows // SPAN
    q_blocks = jnp.transpose(queries.reshape(span_count, SPAN, head_count, key_dim), (0, 2, 1, 3))
    k_blocks = jnp.transpose(keys_norm.reshape(span_count, SPAN, head_count, key_dim), (0, 2, 1, 3))
    v_blocks = jnp.transpose(values.reshape(span_count, SPAN, head_count, value_dim), (0, 2, 1, 3))
    rate_blocks = jnp.transpose(beta_rate.reshape(span_count, SPAN, head_count), (0, 2, 1))
    key_gram = jnp.einsum("nhcd,nhsd->nhcs", k_blocks, k_blocks, preferred_element_type=jnp.float32)
    scores = jnp.einsum("nhcd,nhsd->nhcs", q_blocks, k_blocks, preferred_element_type=jnp.float32)
    row_index = lax.broadcasted_iota(jnp.int32, (SPAN, SPAN), 0)
    col_index = lax.broadcasted_iota(jnp.int32, (SPAN, SPAN), 1)
    lower_part = jnp.where(col_index < row_index, rate_blocks[..., None] * key_gram, 0.0)
    inverse = unit_lower_inverse(lower_part, SPAN)
    k_float = k_blocks.astype(jnp.float32)
    right_side = rate_blocks[..., None] * jnp.concatenate(
        (k_float, v_blocks.astype(jnp.float32)), axis=-1
    )
    solved = jnp.einsum("nhcs,nhsd->nhcd", inverse, right_side, precision=PRECISE)
    w_factor = solved[..., :key_dim]
    u_factor = solved[..., key_dim:]
    identity = jnp.eye(key_dim, dtype=jnp.float32)
    transition = identity - jnp.einsum("nhcd,nhce->nhde", k_float, w_factor, precision=PRECISE)
    written = jnp.einsum("nhcd,nhce->nhde", k_float, u_factor, precision=PRECISE)
    masked = jnp.where(col_index <= row_index, scores, 0.0)
    q_adjusted = q_blocks.astype(jnp.float32) - jnp.einsum(
        "nhcs,nhsd->nhcd", masked, w_factor, precision=PRECISE
    )
    local_part = jnp.einsum("nhcs,nhse->nhce", masked, u_factor, precision=PRECISE)

    def span_step(running, inputs):
        reach, offset = running
        step_map, step_add, adjusted, local_block = inputs
        lead_term = jnp.einsum("hcd,hde->che", adjusted, reach, precision=PRECISE)
        known_term = jnp.einsum(
            "hcd,hde->che", adjusted, offset, precision=PRECISE
        ) + jnp.transpose(local_block, (1, 0, 2))
        return (compose((reach, offset), (step_map, step_add)), (lead_term, known_term))

    ident_map = jnp.broadcast_to(identity, (head_count, key_dim, key_dim))
    zero_add = jnp.zeros((head_count, key_dim, value_dim), jnp.float32)
    device_pair, span_terms = lax.scan(
        span_step, (ident_map, zero_add), (transition, written, q_adjusted, local_part)
    )
    dev_map, dev_add = device_pair
    lead_all, known_all = span_terms
    prior_map, prior_add = prefix(
        (dev_map, dev_add), ("seq", "blk"), compose, (ident_map, zero_add)
    )
    raw_out = known_all + jnp.einsum("nchd,hde->nche", lead_all, prior_add, precision=PRECISE)
    mean_sq = jnp.mean(raw_out * raw_out, axis=-1, keepdims=True)
    normed = raw_out * lax.rsqrt(mean_sq + 1e-05) * out_gain
    return normed.reshape(tok_rows, head_count * value_dim).astype(jnp.bfloat16)


def solution(mesh):
    placed = (
        P(("groups", "seq", "blk"), "hd"),
        P(("groups", "seq", "blk"), "hd"),
        P(("groups", "seq", "blk"), "hd"),
        P(("groups", "seq", "blk"), "hd"),
        P(None, None, "hd"),
        P(),
    )
    return jax.shard_map(
        on_device,
        mesh=mesh,
        in_specs=placed,
        out_specs=P(("groups", "seq", "blk"), "hd"),
        check_vma=False,
    )
```

profile of v0, /device:TPU:0, one launch (start us, length us, event | category | flops | bytes accessed | tf_op | source)
XLA Modules:
  0.0 310.2 jit_solution(18188878677361247098)
XLA Ops:
  8.0 4.8 %collective-permute-start = (bf16[3,3,1024]{2,1,0:T(4,128)(2,1)S(1)}, bf16[3,3,1024]{2,1,0:T(4,128)(2,1)S(1)}, u32[]{:S(2)}, u32[]{:S(2)}) collective-permute-start(bf16[3,3,1024]{2,1,0:T(4,128)(2,1)S(1)} %pad_maximum_fusion), channel_id=1, source_target_pairs={{0,2},{2,4},{4,6},{6,8},{8,10},{10,12},{12,14},{1,3},{3,5},{5,7},{... | collective-permute-start | bytes 55304 | tf_op jit(solution)/shard_map/ppermute | solution.py:15
  16.4 2.6 multiply_bitcast_fusion
  20.3 2.1 copy.44
  24.2 2.7 fusion.64
  26.9 2.3 fusion.95
  29.3 3.2 %add_add_fusion = f32[8,8,64,64]{3,2,1,0:T(8,128)S(1)} fusion(f32[8,8,64,64]{3,2,1,0:T(8,128)S(1)} %fusion.64, f32[8,8,64,64]{3,2,1,0:T(8,128)S(1)} %fusion.94, f32[8,8,64]{2,1,0:T(8,128)S(1)} %bitcast.163, f32[64,64]{1,0:T(8,128)S(1)} %get-tuple-element.252, pred[64,64]{1,0:T(8,128)(4,1)S(1)} %get-tuple-element.251), kind=kOutput, calls=%fused_computation.85 | convolution fusion | flops 203685888 | bytes 3182592 | tf_op jit(solution)/shard_map/nhcs,nhst->nhct/dot_general | solution.py:59
  32.5 2.3 fusion.96
  34.8 2.6 convolution_add_fusion.4
  37.4 2.2 fusion.98
  39.6 2.3 fusion.97
  41.9 2.3 fusion.99
  44.2 2.4 convolution_add_fusion.3
  52.3 2.3 fusion.100
  54.6 4.7 %fusion.32 = f32[8,8,64,256]{3,2,1,0:T(8,128)S(1)} fusion(bf16[8,8,64,128]{3,2,1,0:T(8,128)(2,1)S(1)} %bitcast.157, bf16[8,8,64,128]{3,2,1,0:T(8,128)(2,1)S(1)} %fusion.69, f32[8,8,64]{2,1,0:T(8,128)S(1)} %bitcast.164, f32[8,8,64,64]{3,2,1,0:T(8,128)S(1)} %convolution_add_fusion.3, f32[8,8,64,64]{3,2,1,0:T(8,128)S(1)} %fusion.100), kind=kOutput, calls=%fused_computation.36 | convolution fusion | flops 810811392 | bytes 8404992 | tf_op jit(solution)/shard_map/nhcs,nhsd->nhcd/dot_general | solution.py:98
  59.3 4.1 %fusion.50 = f32[8,8,64,128]{3,2,1,0:T(8,128)} fusion(f32[8,8,64,256]{3,2,1,0:T(8,128)S(1)} %fusion.32, f32[8,8,64,64]{3,2,1,0:T(8,128)S(1)} %fusion.70, pred[64,64]{1,0:T(8,128)(4,1)S(1)} %iota_compare_fusion.1), kind=kOutput, calls=%fused_computation.76 | convolution fusion | flops 402915328 | bytes 6299648 | tf_op jit(solution)/shard_map/nhcs,nhse->nhce/dot_general | solution.py:108
  63.5 2.4 convert_subtract_fusion
  65.9 3.5 %fusion.52 = f32[8,8,128,128]{3,2,1,0:T(8,128)} fusion(bf16[8,8,64,128]{3,2,1,0:T(8,128)(2,1)S(1)} %fusion.69, f32[8,8,64,256]{3,2,1,0:T(8,128)S(1)} %fusion.32), kind=kOutput, calls=%fused_computation.78 | convolution fusion | flops 805306368 | bytes 7340032 | tf_op jit(solution)/shard_map/nhcd,nhce->nhde/dot_general | solution.py:103
  69.4 3.5 %convolution_subtract_fusion = f32[8,8,128,128]{3,2,1,0:T(8,128)} fusion(bf16[8,8,64,128]{3,2,1,0:T(8,128)(2,1)S(1)} %fusion.69, f32[128,128]{1,0:T(8,128)S(1)} %fusion.86, f32[8,8,64,256]{3,2,1,0:T(8,128)S(1)} %fusion.32), kind=kOutput, calls=%fused_computation.39 | convolution fusion | flops 806354944 | bytes 7405568 | tf_op jit(solution)/shard_map/nhcd,nhce->nhde/dot_general | solution.py:102
  73.0 57.9 %while.31 = (s32[]{:T(128)}, f32[8,128,128]{2,1,0:T(8,128)S(1)}, f32[8,128,128]{2,1,0:T(8,128)S(1)}, f32[8,64,8,128]{3,1,0,2:T(8,128)}, f32[8,64,8,128]{3,1,0,2:...) while((s32[]{:T(128)}, f32[8,128,128]{2,1,0:T(8,128)S(1)}, ...), condition=%wide.region_2.3_spmd.clone, body=%wide.region_1.2_spmd.clone.sunk | while | flops 604438528 | bytes 8130168 | solution.py:121
  73.0 2.3 fusion.151
  80.3 2.2 fusion.151
  87.5 2.2 fusion.151
  94.7 2.3 fusion.151
  102.0 2.2 fusion.151
  109.2 2.2 fusion.151
  116.4 2.2 fusion.151
  123.7 2.3 fusion.151
  132.5 74.4 %all-gather.5.cloned.1.call-done = f32[64,128,128]{2,1,0:T(8,128)} async-done(((f32[8,128,128]{2,1,0:T(8,128)}), f32[64,128,128]{2,1,0:T(8,128)}) %all-gather.5.cloned.1.call-update) | async-done | bytes 4194320 | tf_op jit(solution)/shard_map/all_gather | solution.py:20
  206.9 73.8 %all-gather.7.cloned.1.call-done = f32[64,128,128]{2,1,0:T(8,128)} async-done(((f32[8,128,128]{2,1,0:T(8,128)}), f32[64,128,128]{2,1,0:T(8,128)}) %all-gather.7.cloned.1.call-update) | async-done | bytes 4194320 | tf_op jit(solution)/shard_map/all_gather | solution.py:20
  280.7 15.5 %while.32 = (s32[]{:T(128)}, f32[8,128,128]{2,1,0:T(8,128)S(1)}, s32[]{:T(128)}, f32[8,8,128,128]{3,2,1,0:T(8,128)}, f32[8,8,128,128]{3,2,1,0:T(8,128)}, /*index=5*/s32[]{:T(128)}, s32[]{:T(128)}) while((s32[]{:T(128)}, f32[8,128,128]{2,1,0:T(8,128)S(1)}, s32[]{:T(128)}, f32[8,8,128,128]{3,2,1,0:T(8,128)}, ...), condition=%wide.region_4.5_spmd.clone, body=%wide.region_3.4_spmd.clone.sunk | while | flops 201850880 | bytes 3672671 | solution.py:32
  282.7 1.9 fusion.154
  296.3 3.6 %fusion.101 = f32[8,128,512]{1,2,0:S(1)} fusion(f32[8,128,128]{2,1,0:T(8,128)S(1)} %get-tuple-element.152, f32[8,128,512]{1,2,0:T(8,128)} %bitcast.25), kind=kOutput, calls=%fused_computation.143 | convolution fusion | flops 805306368 | bytes 4718592
  (109 shorter events, 71.4 us)
Async XLA Ops:
  6.5 200.4 %all-gather.5.cloned.1.call-start = ((), (), s32[]{:S(2)}) async-start(), calls=%async_computation | async-start | bytes 4718592 | tf_op jit(solution)/shard_map/all_gather | solution.py:20
  8.0 6.8 %collective-permute-start = (bf16[3,3,1024]{2,1,0:T(4,128)(2,1)S(1)}, bf16[3,3,1024]{2,1,0:T(4,128)(2,1)S(1)}, u32[]{:S(2)}, u32[]{:S(2)}) collective-permute-start(bf16[3,3,1024]{2,1,0:T(4,128)(2,1)S(1)} %pad_maximum_fusion), channel_id=1, source_target_pairs={{0,2},{2,4},{4,6},{6,8},{8,10},{10,12},{12,14},{1,3},{3,5},{5,7},{... | collective-permute-start | bytes 55304 | tf_op jit(solution)/shard_map/ppermute | solution.py:15
  44.2 2.4 copy-start.3
  48.5 1.2 copy-start.4
  130.9 0.8 copy-start
  130.9 1.0 copy-start.1
  131.7 149.0 %all-gather.7.cloned.1.call-start = ((), (), s32[]{:S(2)}) async-start(), calls=%async_computation.1 | async-start | bytes 4718592 | tf_op jit(solution)/shard_map/all_gather | solution.py:20
  296.3 3.6 %copy-start.2 = (f32[8,64,8,128]{3,1,0,2:T(8,128)S(1)}, f32[8,64,8,128]{3,1,0,2:T(8,128)}, u32[]{:S(2)}) copy-start(f32[8,64,8,128]{3,1,0,2:T(8,128)} %get-tuple-element.149) | copy-start | bytes 6291460
  299.9 0.7 copy-start.5
Sparse Core Ops, SparseCore 0:
  131.8 75.0 all-gather.4
  209.0 71.6 all-gather.6
where the time goes:
time: 315 us; the launch traced here: 310 us
  waiting for transfers between devices  149 us (47%)
  matrix products  120 us (38%)
  between operations  13.9 us (4%)
  local copies, waits for them, and re-layouts  11.2 us (4%)
  other arithmetic  10.8 us (3%)
  starting transfers between devices  4.89 us (2%)
    all_gather x2, waiting for transfers between devices, prefix(): everything = jax.tree.map(lambda part: lax.all_gather(part, axis), array)  148 us
    dot_general x16, matrix products, compose(): jnp.einsum('hde,hef->hdf', late_map, early_add, precision=PRECISE)  29.7 us
    dot_general x8, matrix products, span_step(): jnp.einsum('hcd,hde->che', adjusted, offset, precision=PRECISE)  18 us
    dot_general x8, matrix products, compose(): jnp.einsum('hde,hef->hdf', late_map, early_map, precision=PRECISE)  13.6 us
    dot_general x5, matrix products, unit_lower_inverse(): jnp.einsum('nhcs,nhst->nhct', inverse, power, precision=PRECISE)  12.8 us
    dot_general x5, matrix products, unit_lower_inverse(): power = jnp.einsum('nhcs,nhst->nhct', power, power, precision=PRECISE)  11.8 us
    dot_general x8, matrix products, span_step(): lead_term = jnp.einsum('hcd,hde->che', adjusted, reach, precision=PRECISE)  10.6 us
  transfers between devices with their start and end apart: 3, of which 2 were waited for; matrix products, arithmetic and copies ran while one was open for 1% of the time, Pallas kernels for 0%

commit v1 on v0

v1 whole, which is shorter than its diff:
```python
import functools

import jax
import jax.numpy as jnp
from jax import lax
from jax.experimental import pallas as pl
from jax.experimental.pallas import tpu as pltpu
from jax.sharding import PartitionSpec as P

F32 = jnp.float32
BF16 = jnp.bfloat16
CHUNK = 128
RIM = 16
LEAD = 8
PAIR = 2
SMALL = 16
MESH = pl.DeviceIdType.MESH


def mm(a, b):
    return jnp.dot(a.astype(BF16), b.astype(BF16), preferred_element_type=F32)


def mm_nt(a, b):
    return lax.dot_general(a, b, (((1,), (1,)), ((), ())), preferred_element_type=F32)


def split(x):
    high = x.astype(BF16)
    return high, (x - high.astype(F32)).astype(BF16)


def local_kernel(taps, q_ref, k_ref, v_ref, rim_ref, w_ref, beta_ref,
                 a_ref, b_ref, lead_ref, known_ref, pad):
    step = pl.program_id(0)
    rows = q_ref.shape[0]
    dim = a_ref.shape[-1]
    chunks = rows // CHUNK
    row = lax.broadcasted_iota(jnp.int32, (CHUNK, CHUNK), 0)
    col = lax.broadcasted_iota(jnp.int32, (CHUNK, CHUNK), 1)
    head_lane = lax.broadcasted_iota(jnp.int32, beta_ref.shape, 1)
    zero = jnp.zeros((CHUNK, CHUNK), F32)

    def conv(which, ref, head):
        lanes = slice(head * dim, (head + 1) * dim)
        slot = head * 3 + which
        pad[slot, 0:LEAD] = rim_ref[which, RIM - LEAD:RIM, lanes].astype(F32)
        pad[slot, LEAD:] = ref[:, lanes].astype(F32)
        total = jnp.zeros((rows, dim), F32)
        for tap in range(taps):
            total = total + w_ref[which, tap:tap + 1, lanes] * pad[
                slot, pl.ds(LEAD - taps + 1 + tap, rows)]
        return total / (1.0 + jnp.exp(-total))

    qs, ks, vs, rates = [], [], [], []
    for head in range(PAIR):
        q = conv(0, q_ref, head).astype(BF16)
        k = conv(1, k_ref, head)
        k = (k * lax.rsqrt(jnp.sum(k * k, axis=-1, keepdims=True) + 1e-06)).astype(BF16)
        v = conv(2, v_ref, head).astype(BF16)
        rate = jnp.sum(
            jnp.where(head_lane == step * PAIR + head, beta_ref[...], 0.0), axis=1, keepdims=True)
        for c in range(chunks):
            part = slice(c * CHUNK, (c + 1) * CHUNK)
            qs.append(q[part])
            ks.append(k[part])
            vs.append(v[part])
            rates.append(rate[part])
    both = [mm_nt(jnp.concatenate((q, k), axis=0), k) for q, k in zip(qs, ks)]
    scores = [jnp.where(col <= row, x[:CHUNK], 0.0) for x in both]
    lower = [jnp.where(col < row, r * x[CHUNK:], 0.0) for r, x in zip(rates, both)]
    near = row // SMALL == col // SMALL
    power = [jnp.where(near, x, zero) for x in lower]
    rest = [-x for x in power]
    size = 2
    while size < SMALL:
        power = [mm(x, x) for x in power]
        rest = [x + y + mm(x, y) for x, y in zip(rest, power)]
        size *= 2
    size = SMALL
    while size < CHUNK:
        band = (row // (2 * size) == col // (2 * size)) & (row // size != col // size)
        off = [jnp.where(band, x, zero) for x in lower]
        mid = [x + mm(x, y) for x, y in zip(off, rest)]
        rest = [x - y - mm(x, y) for x, y in zip(rest, mid)]
        size *= 2
    flat = [jnp.sum(jnp.where(row == col, r, 0.0), axis=0, keepdims=True) for r in rates]
    kv = [jnp.concatenate((k, v), axis=1) for k, v in zip(ks, vs)]
    wu = [r * x.astype(F32) + mm(t * f, x) for r, x, t, f in zip(rates, kv, rest, flat)]
    made = [
        mm(jnp.concatenate((s, k.astype(F32).T), axis=0), x)
        for s, k, x in zip(scores, ks, wu)
    ]
    left = [
        jnp.concatenate((q.astype(F32) - x[:CHUNK, :dim], x[CHUNK:, :dim]), axis=0).astype(BF16)
        for q, x in zip(qs, made)
    ]
    eye = jnp.where(row == col, 1.0, 0.0)
    for c in range(chunks):
        part = slice(c * CHUNK, (c + 1) * CHUNK)
        for head in range(PAIR):
            n = head * chunks + c
            x = made[n]
            if c == 0:
                lead_ref[head, part] = left[n][:CHUNK]
                known_ref[head, part] = x[:CHUNK, dim:]
                a_ref[head] = eye - x[CHUNK:, :dim]
                b_ref[head] = x[CHUNK:, dim:]
            else:
                state = jnp.concatenate((a_ref[head], b_ref[head]), axis=1)
                y = mm(left[n], state)
                lead_ref[head, part] = y[:CHUNK, :dim].astype(BF16)
                known_ref[head, part] = y[:CHUNK, dim:] + x[:CHUNK, dim:]
                a_ref[head] = state[:, :dim] - y[CHUNK:, :dim]
                b_ref[head] = state[:, dim:] - y[CHUNK:, dim:] + x[CHUNK:, dim:]


def chain_kernel(seqs, blks, a_ref, b_ref, lead_ref, known_ref, gain_ref, o_ref,
                 came, goes, send_sem, recv_sem):
    heads, dim = a_ref.shape[0], a_ref.shape[-1]
    total = seqs * blks
    here = lax.axis_index("seq") * blks + lax.axis_index("blk")
    after = (here + 1) % total
    ahead = (here + total - 1) % total
    after_id = {"seq": after // blks, "blk": after % blks}
    ahead_id = {"seq": ahead // blks, "blk": ahead % blks}

    barrier = pltpu.get_barrier_semaphore()

    @pl.when(here > 0)
    def _():
        pl.semaphore_signal(barrier, inc=1, device_id=ahead_id, device_id_type=MESH)

    @pl.when(here < total - 1)
    def _():
        pl.semaphore_signal(barrier, inc=1, device_id=after_id, device_id_type=MESH)

    inner = (here > 0) & (here < total - 1)

    @pl.when(inner)
    def _():
        pl.semaphore_wait(barrier, 2)

    @pl.when(jnp.logical_not(inner))
    def _():
        pl.semaphore_wait(barrier, 1)

    def move(head):
        return pltpu.make_async_remote_copy(
            src_ref=goes.at[head], dst_ref=came.at[head],
            send_sem=send_sem.at[head], recv_sem=recv_sem.at[head],
            device_id=after_id, device_id_type=MESH)

    @pl.when(here == 0)
    def _():
        came[...] = jnp.zeros_like(came)

    def visit(head, carry):
        @pl.when(here > 0)
        def _():
            move(head).wait_recv()

        state_high, state_low = split(came[head])

        @pl.when(here < total - 1)
        def _():
            map_high, map_low = split(a_ref[head])
            goes[head] = b_ref[head] + (
                mm(map_high, state_high) + mm(map_high, state_low) + mm(map_low, state_high))
            move(head).start()

        out = known_ref[head] + mm(lead_ref[head], state_high)
        mean_sq = jnp.mean(out * out, axis=-1, keepdims=True)
        out = out * lax.rsqrt(mean_sq + 1e-05) * gain_ref[...]
        o_ref[:, pl.ds(pl.multiple_of(head * dim, dim), dim)] = out.astype(o_ref.dtype)
        return carry

    lax.fori_loop(0, heads, visit, 0)

    def close(head, carry):
        @pl.when(here < total - 1)
        def _():
            move(head).wait_send()
        return carry

    lax.fori_loop(0, heads, close, 0)


def on_device(query_raw, key_raw, value_raw, beta_rate, conv_weight, out_gain):
    rows, width = query_raw.shape
    heads = beta_rate.shape[1]
    dim = width // heads
    taps = conv_weight.shape[1]
    seqs, blks = lax.axis_size("seq"), lax.axis_size("blk")
    total = seqs * blks
    ends = jnp.stack([x[rows - RIM:] for x in (query_raw, key_raw, value_raw)])
    rim = lax.ppermute(ends, ("seq", "blk"), [(i, i + 1) for i in range(total - 1)])
    wide = PAIR * dim
    raw_spec = pl.BlockSpec((rows, wide), lambda i: (0, i))
    square = pl.BlockSpec((PAIR, dim, dim), lambda i: (i, 0, 0))
    tall = pl.BlockSpec((PAIR, rows, dim), lambda i: (i, 0, 0))
    maps, adds, lead, known = pl.pallas_call(
        functools.partial(local_kernel, taps),
        name="local_part",
        grid=(heads // PAIR,),
        out_shape=(
            jax.ShapeDtypeStruct((heads, dim, dim), F32),
            jax.ShapeDtypeStruct((heads, dim, dim), F32),
            jax.ShapeDtypeStruct((heads, rows, dim), BF16),
            jax.ShapeDtypeStruct((heads, rows, dim), F32),
        ),
        in_specs=[
            raw_spec, raw_spec, raw_spec,
            pl.BlockSpec((3, RIM, wide), lambda i: (0, 0, i)),
            pl.BlockSpec((3, taps, wide), lambda i: (0, 0, i)),
            pl.BlockSpec((rows, heads), lambda i: (0, 0)),
        ],
        out_specs=(square, square, tall, tall),
        scratch_shapes=[pltpu.VMEM((3 * PAIR, rows + LEAD, dim), F32)],
        compiler_params=pltpu.CompilerParams(vmem_limit_bytes=40 << 20),
    )(query_raw, key_raw, value_raw, rim, conv_weight, beta_rate)
    vmem = pl.BlockSpec(memory_space=pltpu.VMEM)
    return pl.pallas_call(
        functools.partial(chain_kernel, seqs, blks),
        name="chain_part",
        out_shape=jax.ShapeDtypeStruct((rows, width), BF16),
        in_specs=[vmem] * 5,
        out_specs=vmem,
        scratch_shapes=[
            pltpu.VMEM((heads, dim, dim), F32),
            pltpu.VMEM((heads, dim, dim), F32),
            pltpu.SemaphoreType.DMA((heads,)),
            pltpu.SemaphoreType.DMA((heads,)),
        ],
        compiler_params=pltpu.CompilerParams(
            collective_id=0, has_side_effects=True, vmem_limit_bytes=40 << 20),
    )(maps, adds, lead, known, out_gain.reshape(1, dim))


def solution(mesh):
    placed = (
        P(("groups", "seq", "blk"), "hd"),
        P(("groups", "seq", "blk"), "hd"),
        P(("groups", "seq", "blk"), "hd"),
        P(("groups", "seq", "blk"), "hd"),
        P(None, None, "hd"),
        P(),
    )
    return jax.shard_map(
        on_device,
        mesh=mesh,
        in_specs=placed,
        out_specs=P(("groups", "seq", "blk"), "hd"),
        check_vma=False,
    )
```

time: 315 us -> 65 us (0.21)
  the two profiles are of different devices: /device:TPU:0 before, /device:TPU:30 now
where the time goes in v1:
time: 65 us; the launch traced here: 64.5 us
  Pallas kernels  50.9 us (78%)
  local copies, waits for them, and re-layouts  7.84 us (12%)
  waiting for transfers between devices  4.36 us (7%)
  starting transfers between devices  1.29 us (2%)
    pallas_call x1, Pallas kernels, on_device(): pl.pallas_call(functools.partial(chain_kernel, seqs, blks), name='chain_p...  34.2 us
    pallas_call x1, Pallas kernels, on_device(): pl.pallas_call(functools.partial(local_kernel, taps), name='local_part',...  16.7 us
    unnamed x12, local copies, waits for them, and re-layouts  6.29 us
    ppermute x1, waiting for transfers between devices, on_device(): lax.ppermute(ends, ('seq', 'blk'), [(i, i + 1) for i in range(total - 1)])  4.36 us
    another operation x2, local copies, waits for them, and re-layouts, on_device(): ends = jnp.stack([x[rows - RIM:] for x in (query_raw, key_raw, value_raw)])  1.55 us
  transfers between devices with their start and end apart: 1, of which 1 were waited for; matrix products, arithmetic and copies ran while one was open for 1% of the time, Pallas kernels for 0%

profile of v1, /device:TPU:30, one launch (start us, length us, event | category | flops | bytes accessed | tf_op | source)
XLA Modules:
  0.0 64.5 jit_solution(14225650034435234000)
XLA Ops:
  0.0 0.8 %slice_bitcast_fusion.2 = bf16[1,16,1024]{2,1,0:T(8,128)(2,1)S(1)} fusion(bf16[512,1024]{1,0:T(8,128)(2,1)} %q_ref.1), kind=kLoop, calls=%fused_computation.3 | loop fusion | bytes 65536 | tf_op jit(solution)/shard_map/stack | solution.py:196
  0.8 0.0 copy-start.4
  0.8 0.8 %slice_bitcast_fusion = (bf16[1,16,1024]{2,1,0:T(8,128)(2,1)S(1)}, bf16[1,16,1024]{2,1,0:T(8,128)(2,1)S(1)}) fusion(bf16[512,1024]{1,0:T(8,128)(2,1)} %v_ref.1, bf16[512,1024]{1,0:T(8,128)(2,1)} %k_ref.1), kind=kLoop, calls=%fused_computation.1 | loop fusion | bytes 131072 | tf_op jit(solution)/shard_map/stack | solution.py:196
  1.6 1.3 %collective-permute-start = (bf16[3,16,1024]{2,1,0:T(8,128)(2,1)S(1)}, bf16[3,16,1024]{2,1,0:T(8,128)(2,1)S(1)}, u32[]{:S(2)}, u32[]{:S(2)}) collective-permute-start(bf16[3,16,1024]{2,1,0:T(8,128)(2,1)S(1)} %pad_maximum_fusion), channel_id=1, source_target_pairs={{0,2},{2,4},{4,6},{6,8},{8,10},{10,12},{12,14},{1,3},{3,5},{5,7},{... | collective-permute-start | bytes 294920 | tf_op jit(solution)/shard_map/ppermute | solution.py:197
  2.9 0.8 %copy.7.beta_ref = f32[512,8]{1,0:T(8,128)S(1)} copy(f32[512,8]{0,1:T(8,128)} %param.9) | data formatting | bytes 32768 | tf_op args[3]
  3.7 4.4 %collective-permute-done.rim_ref = bf16[3,16,1024]{2,1,0:T(8,128)(2,1)S(1)} collective-permute-done((bf16[3,16,1024]{2,1,0:T(8,128)(2,1)S(1)}, bf16[3,16,1024]{2,1,0:T(8,128)(2,1)S(1)}, u32[]{:S(2)}, u32[]{:S(2)}) %collective-permute-start) | collective-permute-done | bytes 98336 | tf_op jit(solution)/shard_map/ppermute | solution.py:197
  8.1 0.0 copy-start
  8.1 1.2 %copy-done = bf16[512,1024]{1,0:T(8,128)(2,1)S(1)} copy-done((bf16[512,1024]{1,0:T(8,128)(2,1)S(1)}, bf16[512,1024]{1,0:T(8,128)(2,1)}, u32[]{:S(2)}) %copy-start) | copy-done | bytes 1048600
  9.3 0.0 copy-start.1
  9.3 1.2 %copy-done.1 = bf16[512,1024]{1,0:T(8,128)(2,1)S(1)} copy-done((bf16[512,1024]{1,0:T(8,128)(2,1)S(1)}, bf16[512,1024]{1,0:T(8,128)(2,1)}, u32[]{:S(2)}) %copy-start.1) | copy-done | bytes 1048600
  10.5 0.0 copy-start.2
  10.5 1.2 %copy-done.2 = bf16[512,1024]{1,0:T(8,128)(2,1)S(1)} copy-done((bf16[512,1024]{1,0:T(8,128)(2,1)S(1)}, bf16[512,1024]{1,0:T(8,128)(2,1)}, u32[]{:S(2)}) %copy-start.2) | copy-done | bytes 1048600
  11.8 0.0 copy-start.3
  11.8 0.8 %copy-done.3 = f32[3,4,1024]{2,1,0:T(4,128)S(1)} copy-done((f32[3,4,1024]{2,1,0:T(4,128)S(1)}, f32[3,4,1024]{2,1,0:T(4,128)}, u32[]{:S(2)}) %copy-start.3) | copy-done | bytes 49176
  12.6 16.7 %local_part.1 = (f32[8,128,128]{2,1,0:T(8,128)S(1)}, f32[8,128,128]{2,1,0:T(8,128)S(1)}, bf16[8,512,128]{2,1,0:T(8,128)(2,1)S(1)}, f32[8,512,128]{2,1,0:T(8,128)S(1)}) custom-call(bf16[512,1024]{1,0:T(8,128)(2,1)S(1)} %copy-done, bf16[512,1024]{1,0:T(8,128)(2,1)S(1)} %copy-done.1, bf16[512,1024]{1,0:T(8,128)(2,1)S(1)} %copy-done.2, ...), custom_call_target="tpu_custom_call" | custom-call | tf_op jit(solution)/shard_map/local_part/pallas_call | solution.py:202
  29.2 0.0 copy-done.4
  29.2 34.2 %chain_part.1 = bf16[512,1024]{1,0:T(8,128)(2,1)S(1)} custom-call(f32[8,128,128]{2,1,0:T(8,128)S(1)} %get-tuple-element.9.a_ref, f32[8,128,128]{2,1,0:T(8,128)S(1)} %get-tuple-element.10.b_ref, bf16[8,512,128]{2,1,0:T(8,128)(2,1)S(1)} %get-tuple-element.11.lead_ref, f32[8,512,128]{2,1,0:T(8,128)S(1)} %get-tuple-element.12.known_ref, f32[1,128]{1,0:T(1,128)S(1)} %bitcast.7), custom_call_target="tpu_custom_call" | custom-call | tf_op jit(solution)/shard_map/chain_part/pallas_call | solution.py:223
  63.5 1.0 %copy.9 = bf16[512,1024]{1,0:T(8,128)(2,1)} copy(bf16[512,1024]{1,0:T(8,128)(2,1)S(1)} %chain_part.1) | data formatting | bytes 2097152
  (1 shorter events, 0.0 us)
Async XLA Ops:
  0.8 28.5 %copy-start.4 = (f32[128]{0:T(128)S(1)}, f32[128]{0:T(128)}, u32[]{:S(2)}) copy-start(f32[128]{0:T(128)} %param.11) | copy-start | bytes 1540
  1.6 6.5 %collective-permute-start = (bf16[3,16,1024]{2,1,0:T(8,128)(2,1)S(1)}, bf16[3,16,1024]{2,1,0:T(8,128)(2,1)S(1)}, u32[]{:S(2)}, u32[]{:S(2)}) collective-permute-start(bf16[3,16,1024]{2,1,0:T(8,128)(2,1)S(1)} %pad_maximum_fusion), channel_id=1, source_target_pairs={{0,2},{2,4},{4,6},{6,8},{8,10},{10,12},{12,14},{1,3},{3,5},{5,7},{... | collective-permute-start | bytes 294920 | tf_op jit(solution)/shard_map/ppermute | solution.py:197
  8.1 1.2 %copy-start = (bf16[512,1024]{1,0:T(8,128)(2,1)S(1)}, bf16[512,1024]{1,0:T(8,128)(2,1)}, u32[]{:S(2)}) copy-start(bf16[512,1024]{1,0:T(8,128)(2,1)} %q_ref.1) | copy-start | bytes 3145732
  9.3 1.2 %copy-start.1 = (bf16[512,1024]{1,0:T(8,128)(2,1)S(1)}, bf16[512,1024]{1,0:T(8,128)(2,1)}, u32[]{:S(2)}) copy-start(bf16[512,1024]{1,0:T(8,128)(2,1)} %k_ref.1) | copy-start | bytes 3145732
  10.5 1.2 %copy-start.2 = (bf16[512,1024]{1,0:T(8,128)(2,1)S(1)}, bf16[512,1024]{1,0:T(8,128)(2,1)}, u32[]{:S(2)}) copy-start(bf16[512,1024]{1,0:T(8,128)(2,1)} %v_ref.1) | copy-start | bytes 3145732
  11.8 0.8 %copy-start.3 = (f32[3,4,1024]{2,1,0:T(4,128)S(1)}, f32[3,4,1024]{2,1,0:T(4,128)}, u32[]{:S(2)}) copy-start(f32[3,4,1024]{2,1,0:T(4,128)} %w_ref.1) | copy-start | bytes 147460

commit v2 on v1

v2 whole, which is shorter than its diff:
```python
import functools

import jax
import jax.numpy as jnp
from jax import lax
from jax.experimental import pallas as pl
from jax.experimental.pallas import tpu as pltpu
from jax.sharding import PartitionSpec as P

F32 = jnp.float32
BF16 = jnp.bfloat16
CHUNK = 128
RIM = 16
LEAD = 8
PAIR = 2
SMALL = 16
MESH = pl.DeviceIdType.MESH


def mm(a, b):
    return jnp.dot(a.astype(BF16), b.astype(BF16), preferred_element_type=F32)


def mm_nt(a, b):
    return lax.dot_general(a, b, (((1,), (1,)), ((), ())), preferred_element_type=F32)


def split(x):
    high = x.astype(BF16)
    return high, (x - high.astype(F32)).astype(BF16)


def mm3(a, b):
    a_high, a_low = split(a)
    b_high, b_low = split(b)
    return mm(a_high, b_high) + mm(a_high, b_low) + mm(a_low, b_high)


def layer_kernel(seqs, blks, taps, q_hbm, k_hbm, v_hbm, w_ref, beta_ref, gain_ref, o_ref,
                 raw, rim, pad, keys, wu_ref, state_ref, a_ref, b_ref, lead_ref, known_ref,
                 came, goes, load_sem, rim_send, rim_recv, send_sem, recv_sem):
    rows = q_hbm.shape[0]
    heads, dim = a_ref.shape[0], a_ref.shape[-1]
    chunks = rows // CHUNK
    pairs = heads // PAIR
    total = seqs * blks
    here = lax.axis_index("seq") * blks + lax.axis_index("blk")
    after = (here + 1) % total
    ahead = (here + total - 1) % total
    after_id = {"seq": after // blks, "blk": after % blks}
    ahead_id = {"seq": ahead // blks, "blk": ahead % blks}
    has_ahead = here > 0
    has_after = here < total - 1
    sources = (q_hbm, k_hbm, v_hbm)

    def load(which):
        return pltpu.make_async_copy(sources[which], raw.at[which], load_sem.at[which])

    def rim_move(which):
        return pltpu.make_async_remote_copy(
            src_ref=sources[which].at[pl.ds(rows - RIM, RIM)], dst_ref=rim.at[which],
            send_sem=rim_send.at[which], recv_sem=rim_recv.at[which],
            device_id=after_id, device_id_type=MESH)

    def move(head):
        return pltpu.make_async_remote_copy(
            src_ref=goes.at[head], dst_ref=came.at[head],
            send_sem=send_sem.at[head], recv_sem=recv_sem.at[head],
            device_id=after_id, device_id_type=MESH)

    barrier = pltpu.get_barrier_semaphore()

    @pl.when(has_ahead)
    def _():
        pl.semaphore_signal(barrier, inc=1, device_id=ahead_id, device_id_type=MESH)

    @pl.when(has_after)
    def _():
        pl.semaphore_signal(barrier, inc=1, device_id=after_id, device_id_type=MESH)

    for which in (1, 2, 0):
        load(which).start()

    @pl.when(here == 0)
    def _():
        came[...] = jnp.zeros_like(came)
        rim[...] = jnp.zeros_like(rim)

    inner = has_ahead & has_after

    @pl.when(inner)
    def _():
        pl.semaphore_wait(barrier, 2)

    @pl.when(jnp.logical_not(inner))
    def _():
        pl.semaphore_wait(barrier, 1)

    @pl.when(has_after)
    def _():
        for which in (1, 2, 0):
            rim_move(which).start()

    for which in (1, 2, 0):
        load(which).wait()

    @pl.when(has_ahead)
    def _():
        for which in (1, 2, 0):
            rim_move(which).wait_recv()

    row = lax.broadcasted_iota(jnp.int32, (CHUNK, CHUNK), 0)
    col = lax.broadcasted_iota(jnp.int32, (CHUNK, CHUNK), 1)
    head_lane = lax.broadcasted_iota(jnp.int32, beta_ref.shape, 1)
    eye = jnp.where(row == col, 1.0, 0.0)

    def lanes_of(head):
        return pl.ds(pl.multiple_of(head * dim, dim), dim)

    def conv(which, head, slot):
        lanes = lanes_of(head)
        pad[slot, 0:LEAD] = rim[which, RIM - LEAD:RIM, lanes].astype(F32)
        pad[slot, LEAD:] = raw[which, :, lanes].astype(F32)
        summed = jnp.zeros((rows, dim), F32)
        for tap in range(taps):
            summed = summed + w_ref[which, tap:tap + 1, lanes] * pad[
                slot, pl.ds(LEAD - taps + 1 + tap, rows)]
        return summed / (1.0 + jnp.exp(-summed))

    def maps_of(pair):
        ks, vs, rates = [], [], []
        for lane in range(PAIR):
            head = pair * PAIR + lane
            k = conv(1, head, lane * 2)
            k = (k * lax.rsqrt(jnp.sum(k * k, axis=-1, keepdims=True) + 1e-06)).astype(BF16)
            keys[:, lanes_of(head)] = k
            v = conv(2, head, lane * 2 + 1).astype(BF16)
            rate = jnp.sum(
                jnp.where(head_lane == head, beta_ref[...], 0.0), axis=1, keepdims=True)
            for c in range(chunks):
                part = slice(c * CHUNK, (c + 1) * CHUNK)
                ks.append(k[part])
                vs.append(v[part])
                rates.append(rate[part])
        lower = [jnp.where(col < row, r * mm_nt(k, k), 0.0) for r, k in zip(rates, ks)]
        near = row // SMALL == col // SMALL
        power = [jnp.where(near, x, 0.0) for x in lower]
        rest = [-x for x in power]
        size = 2
        while size < SMALL:
            power = [mm(x, x) for x in power]
            rest = [x + y + mm(x, y) for x, y in zip(rest, power)]
            size *= 2
        size = SMALL
        while size < CHUNK:
            band = (row // (2 * size) == col // (2 * size)) & (row // size != col // size)
            off = [jnp.where(band, x, 0.0) for x in lower]
            mid = [x + mm(x, y) for x, y in zip(off, rest)]
            rest = [x - y - mm(x, y) for x, y in zip(rest, mid)]
            size *= 2
        flat = [jnp.sum(jnp.where(row == col, r, 0.0), axis=0, keepdims=True) for r in rates]
        kv = [jnp.concatenate((k, v), axis=1) for k, v in zip(ks, vs)]
        wu = [r * x.astype(F32) + mm(t * f, x) for r, x, t, f in zip(rates, kv, rest, flat)]
        made = []
        for k, x in zip(ks, wu):
            turned = k.astype(F32).T.astype(BF16)
            high, low = split(x)
            made.append(mm(turned, high) + mm(turned, low))
        states = [jnp.concatenate((eye, jnp.zeros((dim, dim), F32)), axis=1)] * PAIR
        for c in range(chunks):
            part = slice(c * CHUNK, (c + 1) * CHUNK)
            for lane in range(PAIR):
                head = pair * PAIR + lane
                x = made[lane * chunks + c]
                wu_ref[head, part] = wu[lane * chunks + c]
                state_ref[head, part] = states[lane]
                step = x[:, :dim] if c else None
                written = jnp.concatenate((jnp.zeros((dim, dim), F32), x[:, dim:]), axis=1)
                if c:
                    states[lane] = states[lane] - mm(step, states[lane]) + written
                else:
                    states[lane] = jnp.concatenate((eye - x[:, :dim], x[:, dim:]), axis=1)
        for lane in range(PAIR):
            a_ref[pair * PAIR + lane] = states[lane][:, :dim]
            b_ref[pair * PAIR + lane] = states[lane][:, dim:]

    def pass_on(pair):
        for lane in range(PAIR):
            head = pair * PAIR + lane

            @pl.when(has_ahead)
            def _():
                move(head).wait_recv()

            @pl.when(has_after)
            def _():
                map_high, map_low = split(a_ref[head])
                state = came[head]
                goes[head] = (b_ref[head] + (mm(map_high, state) + mm(map_low, state))).astype(BF16)
                move(head).start()

    def reads_of(pair):
        for lane in range(PAIR):
            head = pair * PAIR + lane
            q = conv(0, head, lane).astype(BF16)
            for c in range(chunks):
                part = slice(c * CHUNK, (c + 1) * CHUNK)
                scores = jnp.where(col <= row, mm_nt(q[part], keys[part, lanes_of(head)]), 0.0)
                near = mm3(scores, wu_ref[head, part])
                y = mm3(q[part].astype(F32) - near[:, :dim], state_ref[head, part])
                lead_ref[head, part] = y[:, :dim]
                known_ref[head, part] = y[:, dim:] + near[:, dim:]

    def finish(pair):
        for lane in range(PAIR):
            head = pair * PAIR + lane
            high, low = split(lead_ref[head])
            state = came[head]
            out = known_ref[head] + (mm(high, state) + mm(low, state))
            mean_sq = jnp.mean(out * out, axis=-1, keepdims=True)
            out = out * lax.rsqrt(mean_sq + 1e-05) * gain_ref[...]
            o_ref[:, lanes_of(head)] = out.astype(o_ref.dtype)

    def first_part(i, carry):
        maps_of(i)

        @pl.when(i >= here)
        def _():
            pass_on(i - here)
        return carry

    def second_part(i, carry):
        reads_of(i - pairs)

        @pl.when((i >= here) & (i < here + pairs))
        def _():
            pass_on(i - here)

        @pl.when(here <= pairs)
        def _():
            finish(i - pairs)

        @pl.when((here > pairs) & (i >= here))
        def _():
            finish(i - here)
        return carry

    def third_part(i, carry):
        @pl.when(i >= here)
        def _():
            pass_on(i - here)
            finish(i - here)
        return carry

    lax.fori_loop(0, pairs, first_part, 0)
    lax.fori_loop(pairs, 2 * pairs, second_part, 0)
    lax.fori_loop(2 * pairs, here + pairs, third_part, 0)

    @pl.when(has_after)
    def _():
        for which in range(3):
            rim_move(which).wait_send()
        for head in range(heads):
            move(head).wait_send()


def on_device(query_raw, key_raw, value_raw, beta_rate, conv_weight, out_gain):
    rows, width = query_raw.shape
    heads = beta_rate.shape[1]
    dim = width // heads
    taps = conv_weight.shape[1]
    seqs, blks = lax.axis_size("seq"), lax.axis_size("blk")
    far = pl.BlockSpec(memory_space=pltpu.HBM)
    vmem = pl.BlockSpec(memory_space=pltpu.VMEM)
    return pl.pallas_call(
        functools.partial(layer_kernel, seqs, blks, taps),
        name="layer",
        out_shape=jax.ShapeDtypeStruct((rows, width), BF16),
        in_specs=[far, far, far, vmem, vmem, vmem],
        out_specs=vmem,
        scratch_shapes=[
            pltpu.VMEM((3, rows, width), BF16),
            pltpu.VMEM((3, RIM, width), BF16),
            pltpu.VMEM((2 * PAIR, rows + LEAD, dim), F32),
            pltpu.VMEM((rows, width), BF16),
            pltpu.VMEM((heads, rows, 2 * dim), F32),
            pltpu.VMEM((heads, rows, 2 * dim), F32),
            pltpu.VMEM((heads, dim, dim), F32),
            pltpu.VMEM((heads, dim, dim), F32),
            pltpu.VMEM((heads, rows, dim), F32),
            pltpu.VMEM((heads, rows, dim), F32),
            pltpu.VMEM((heads, dim, dim), BF16),
            pltpu.VMEM((heads, dim, dim), BF16),
            pltpu.SemaphoreType.DMA((3,)),
            pltpu.SemaphoreType.DMA((3,)),
            pltpu.SemaphoreType.DMA((3,)),
            pltpu.SemaphoreType.DMA((heads,)),
            pltpu.SemaphoreType.DMA((heads,)),
        ],
        compiler_params=pltpu.CompilerParams(
            collective_id=0, has_side_effects=True, vmem_limit_bytes=56 << 20),
    )(query_raw, key_raw, value_raw, conv_weight, beta_rate, out_gain.reshape(1, dim))


def solution(mesh):
    placed = (
        P(("groups", "seq", "blk"), "hd"),
        P(("groups", "seq", "blk"), "hd"),
        P(("groups", "seq", "blk"), "hd"),
        P(("groups", "seq", "blk"), "hd"),
        P(None, None, "hd"),
        P(),
    )
    return jax.shard_map(
        on_device,
        mesh=mesh,
        in_specs=placed,
        out_specs=P(("groups", "seq", "blk"), "hd"),
        check_vma=False,
    )
```

time: 65 us -> 48 us (0.74)
  the two profiles are of different devices: /device:TPU:30 before, /device:TPU:26 now
where the time goes in v2:
time: 48 us; the launch traced here: 47.8 us
  Pallas kernels  44 us (92%)
  local copies, waits for them, and re-layouts  3.82 us (8%)
    pallas_call x1, Pallas kernels, on_device(): pl.pallas_call(functools.partial(layer_kernel, seqs, blks, taps), name='l...  44 us
    unnamed x2, local copies, waits for them, and re-layouts  3.82 us

profile of v2, /device:TPU:26, one launch (start us, length us, event | category | flops | bytes accessed | tf_op | source)
XLA Modules:
  0.0 47.8 jit_solution(3153613714684794266)
XLA Ops:
  0.0 1.6 %copy.7.beta_ref = f32[512,8]{1,0:T(8,128)} copy(f32[512,8]{0,1:T(8,128)} %param.9) | data formatting | bytes 32768 | tf_op args[3]
  1.6 44.0 %layer.1 = bf16[512,1024]{1,0:T(8,128)(2,1)} custom-call(bf16[512,1024]{1,0:T(8,128)(2,1)} %q_hbm.1, bf16[512,1024]{1,0:T(8,128)(2,1)} %k_hbm.1, bf16[512,1024]{1,0:T(8,128)(2,1)} %v_hbm.1, f32[3,4,1024]{2,1,0:T(4,128)} %w_ref.1, f32[512,8]{1,0:T(8,128)} %copy.7.beta_ref, f32[1,128]{1,0:T(1,128)} %bitcast.1), custom_call_target="tpu_custom_call" | custom-call | tf_op jit(solution)/shard_map/layer/pallas_call | solution.py:275
  45.5 2.3 %copy.9 = bf16[512,1024]{1,0:T(8,128)(2,1)} copy(bf16[512,1024]{1,0:T(8,128)(2,1)} %layer.1) | data formatting | bytes 2097152

commit v3 on v2

--- a/solution.py
+++ b/solution.py
@@ -40,7 +40,7 @@
                  raw, rim, pad, keys, wu_ref, state_ref, a_ref, b_ref, lead_ref, known_ref,
                  came, goes, load_sem, rim_send, rim_recv, send_sem, recv_sem):
     rows = q_hbm.shape[0]
-    heads, dim = a_ref.shape[0], a_ref.shape[-1]
+    heads, dim = b_ref.shape[0], b_ref.shape[-1]
     chunks = rows // CHUNK
     pairs = heads // PAIR
     total = seqs * blks
@@ -101,17 +101,19 @@
         for which in (1, 2, 0):
             rim_move(which).start()
 
-    for which in (1, 2, 0):
+    def arrive(which):
         load(which).wait()
 
-    @pl.when(has_ahead)
-    def _():
-        for which in (1, 2, 0):
+        @pl.when(has_ahead)
+        def _():
             rim_move(which).wait_recv()
+
+    arrive(1)
+    arrive(2)
 
     row = lax.broadcasted_iota(jnp.int32, (CHUNK, CHUNK), 0)
     col = lax.broadcasted_iota(jnp.int32, (CHUNK, CHUNK), 1)
-    head_lane = lax.broadcasted_iota(jnp.int32, beta_ref.shape, 1)
+    head_row = lax.broadcasted_iota(jnp.int32, (heads, CHUNK), 0)
     eye = jnp.where(row == col, 1.0, 0.0)
 
     def lanes_of(head):
@@ -125,32 +127,35 @@
         for tap in range(taps):
             summed = summed + w_ref[which, tap:tap + 1, lanes] * pad[
                 slot, pl.ds(LEAD - taps + 1 + tap, rows)]
-        return summed / (1.0 + jnp.exp(-summed))
+        half = 0.5 * summed
+        return half + half * jnp.tanh(half)
 
     def maps_of(pair):
-        ks, vs, rates = [], [], []
+        ks, vs, rates, flat = [], [], [], []
         for lane in range(PAIR):
             head = pair * PAIR + lane
             k = conv(1, head, lane * 2)
             k = (k * lax.rsqrt(jnp.sum(k * k, axis=-1, keepdims=True) + 1e-06)).astype(BF16)
             keys[:, lanes_of(head)] = k
             v = conv(2, head, lane * 2 + 1).astype(BF16)
-            rate = jnp.sum(
-                jnp.where(head_lane == head, beta_ref[...], 0.0), axis=1, keepdims=True)
             for c in range(chunks):
                 part = slice(c * CHUNK, (c + 1) * CHUNK)
                 ks.append(k[part])
                 vs.append(v[part])
-                rates.append(rate[part])
+                flat.append(jnp.sum(jnp.where(head_row == head, beta_ref[:, part], 0.0), axis=0, keepdims=True))
+                rates.append(jnp.sum(jnp.where(row == col, flat[-1], 0.0), axis=1, keepdims=True))
         lower = [jnp.where(col < row, r * mm_nt(k, k), 0.0) for r, k in zip(rates, ks)]
         near = row // SMALL == col // SMALL
         power = [jnp.where(near, x, 0.0) for x in lower]
         rest = [-x for x in power]
-        size = 2
+        power = [mm(x, x) for x in power]
+        size = 4
         while size < SMALL:
-            power = [mm(x, x) for x in power]
-            rest = [x + y + mm(x, y) for x, y in zip(rest, power)]
+            joint = [mm(jnp.concatenate((x, y), axis=0), y) for x, y in zip(rest, power)]
+            rest = [x + y + z[:CHUNK] for x, y, z in zip(rest, power, joint)]
+            power = [z[CHUNK:] for z in joint]
             size *= 2
+        rest = [x + y + mm(x, y) for x, y in zip(rest, power)]
         size = SMALL
         while size < CHUNK:
             band = (row // (2 * size) == col // (2 * size)) & (row // size != col // size)
@@ -158,14 +163,13 @@
             mid = [x + mm(x, y) for x, y in zip(off, rest)]
             rest = [x - y - mm(x, y) for x, y in zip(rest, mid)]
             size *= 2
-        flat = [jnp.sum(jnp.where(row == col, r, 0.0), axis=0, keepdims=True) for r in rates]
         kv = [jnp.concatenate((k, v), axis=1) for k, v in zip(ks, vs)]
         wu = [r * x.astype(F32) + mm(t * f, x) for r, x, t, f in zip(rates, kv, rest, flat)]
         made = []
         for k, x in zip(ks, wu):
             turned = k.astype(F32).T.astype(BF16)
-            high, low = split(x)
-            made.append(mm(turned, high) + mm(turned, low))
+            made.append(mm(jnp.concatenate((turned, turned), axis=1),
+                           jnp.concatenate(split(x), axis=0)))
         states = [jnp.concatenate((eye, jnp.zeros((dim, dim), F32)), axis=1)] * PAIR
         for c in range(chunks):
             part = slice(c * CHUNK, (c + 1) * CHUNK)
@@ -181,7 +185,7 @@
                 else:
                     states[lane] = jnp.concatenate((eye - x[:, :dim], x[:, dim:]), axis=1)
         for lane in range(PAIR):
-            a_ref[pair * PAIR + lane] = states[lane][:, :dim]
+            a_ref[pair * PAIR + lane] = jnp.concatenate(split(states[lane][:, :dim]), axis=1)
             b_ref[pair * PAIR + lane] = states[lane][:, dim:]
 
     def pass_on(pair):
@@ -194,9 +198,10 @@
 
             @pl.when(has_after)
             def _():
-                map_high, map_low = split(a_ref[head])
                 state = came[head]
-                goes[head] = (b_ref[head] + (mm(map_high, state) + mm(map_low, state))).astype(BF16)
+                goes[head] = (
+                    b_ref[head] + mm(a_ref[head], jnp.concatenate((state, state), axis=0))
+                ).astype(BF16)
                 move(head).start()
 
     def reads_of(pair):
@@ -214,9 +219,10 @@
     def finish(pair):
         for lane in range(PAIR):
             head = pair * PAIR + lane
-            high, low = split(lead_ref[head])
             state = came[head]
-            out = known_ref[head] + (mm(high, state) + mm(low, state))
+            out = known_ref[head] + mm(
+                jnp.concatenate(split(lead_ref[head]), axis=1),
+                jnp.concatenate((state, state), axis=0))
             mean_sq = jnp.mean(out * out, axis=-1, keepdims=True)
             out = out * lax.rsqrt(mean_sq + 1e-05) * gain_ref[...]
             o_ref[:, lanes_of(head)] = out.astype(o_ref.dtype)
@@ -253,6 +259,7 @@
         return carry
 
     lax.fori_loop(0, pairs, first_part, 0)
+    arrive(0)
     lax.fori_loop(pairs, 2 * pairs, second_part, 0)
     lax.fori_loop(2 * pairs, here + pairs, third_part, 0)
 
@@ -285,7 +292,7 @@
             pltpu.VMEM((rows, width), BF16),
             pltpu.VMEM((heads, rows, 2 * dim), F32),
             pltpu.VMEM((heads, rows, 2 * dim), F32),
-            pltpu.VMEM((heads, dim, dim), F32),
+            pltpu.VMEM((heads, dim, 2 * dim), BF16),
             pltpu.VMEM((heads, dim, dim), F32),
             pltpu.VMEM((heads, rows, dim), F32),
             pltpu.VMEM((heads, rows, dim), F32),
@@ -299,7 +306,7 @@
         ],
         compiler_params=pltpu.CompilerParams(
             collective_id=0, has_side_effects=True, vmem_limit_bytes=56 << 20),
-    )(query_raw, key_raw, value_raw, conv_weight, beta_rate, out_gain.reshape(1, dim))
+    )(query_raw, key_raw, value_raw, conv_weight, beta_rate.T, out_gain.reshape(1, dim))
 
 
 def solution(mesh):

time: 48 us -> 44.7 us (0.931)
  Pallas kernels: 44 us -> 42.2 us
  local copies, waits for them, and re-layouts: 3.82 us -> 2.26 us
    pallas_call x1, Pallas kernels: 44 us -> 42.2 us  [on_device(): pl.pallas_call(functools.partial(layer_kernel, seqs, blks, taps), name='l...]
    unnamed x2 -> x1, local copies, waits for them, and re-layouts: 3.82 us -> 2.26 us
where the time goes in v3:
time: 44.7 us; the launch traced here: 44.5 us
  Pallas kernels  42.2 us (94%)
  local copies, waits for them, and re-layouts  2.26 us (5%)
    pallas_call x1, Pallas kernels, on_device(): pl.pallas_call(functools.partial(layer_kernel, seqs, blks, taps), name='l...  42.2 us
    unnamed x1, local copies, waits for them, and re-layouts  2.26 us

profile of v3, /device:TPU:26, one launch (start us, length us, event | category | flops | bytes accessed | tf_op | source)
XLA Modules:
  0.0 44.5 jit_solution(13843888063698375719)
XLA Ops:
  0.0 42.2 %layer.1 = bf16[512,1024]{1,0:T(8,128)(2,1)} custom-call(bf16[512,1024]{1,0:T(8,128)(2,1)} %q_hbm.1, bf16[512,1024]{1,0:T(8,128)(2,1)} %k_hbm.1, bf16[512,1024]{1,0:T(8,128)(2,1)} %v_hbm.1, f32[3,4,1024]{2,1,0:T(4,128)} %w_ref.1, f32[8,512]{1,0:T(8,128)} %bitcast.2, f32[1,128]{1,0:T(1,128)} %bitcast.3), custom_call_target="tpu_custom_call" | custom-call | tf_op jit(solution)/shard_map/layer/pallas_call | solution.py:282
  42.2 2.3 %copy.8 = bf16[512,1024]{1,0:T(8,128)(2,1)} copy(bf16[512,1024]{1,0:T(8,128)(2,1)} %layer.1) | data formatting | bytes 2097152

commit v4 on v3

--- a/solution.py
+++ b/solution.py
@@ -38,13 +38,20 @@
 
 def layer_kernel(seqs, blks, taps, q_hbm, k_hbm, v_hbm, w_ref, beta_ref, gain_ref, o_ref,
                  raw, rim, pad, keys, wu_ref, state_ref, a_ref, b_ref, lead_ref, known_ref,
-                 came, goes, load_sem, rim_send, rim_recv, send_sem, recv_sem):
+                 came, goes, before, onward, row_a, row_b, load_sem, rim_send, rim_recv,
+                 join_send, join_recv, send_sem, recv_sem):
     rows = q_hbm.shape[0]
     heads, dim = b_ref.shape[0], b_ref.shape[-1]
     chunks = rows // CHUNK
     pairs = heads // PAIR
     total = seqs * blks
-    here = lax.axis_index("seq") * blks + lax.axis_index("blk")
+    z, x = lax.axis_index("seq"), lax.axis_index("blk")
+    end = blks - 1
+    here = z * blks + x
+    lag = z + end
+    sends_row = x < end
+    sends_state = (x == end) & (z < seqs - 1)
+    below = (z + 1) % seqs
     after = (here + 1) % total
     ahead = (here + total - 1) % total
     after_id = {"seq": after // blks, "blk": after % blks}
@@ -62,11 +69,17 @@
             send_sem=rim_send.at[which], recv_sem=rim_recv.at[which],
             device_id=after_id, device_id_type=MESH)
 
-    def move(head):
+    def join(head):
+        return pltpu.make_async_remote_copy(
+            src_ref=onward.at[head], dst_ref=before.at[head],
+            send_sem=join_send.at[head], recv_sem=join_recv.at[head],
+            device_id={"seq": z, "blk": (x + 1) % blks}, device_id_type=MESH)
+
+    def move(head, target):
         return pltpu.make_async_remote_copy(
             src_ref=goes.at[head], dst_ref=came.at[head],
-            send_sem=send_sem.at[head], recv_sem=recv_sem.at[head],
-            device_id=after_id, device_id_type=MESH)
+            send_sem=send_sem.at[target, head], recv_sem=recv_sem.at[head],
+            device_id={"seq": below, "blk": target}, device_id_type=MESH)
 
     barrier = pltpu.get_barrier_semaphore()
 
@@ -83,18 +96,29 @@
 
     @pl.when(here == 0)
     def _():
+        rim[...] = jnp.zeros_like(rim)
+
+    @pl.when(z == 0)
+    def _():
         came[...] = jnp.zeros_like(came)
-        rim[...] = jnp.zeros_like(rim)
-
-    inner = has_ahead & has_after
-
-    @pl.when(inner)
-    def _():
-        pl.semaphore_wait(barrier, 2)
-
-    @pl.when(jnp.logical_not(inner))
-    def _():
-        pl.semaphore_wait(barrier, 1)
+
+    extra_up = (x > 0) & (z > 0)
+
+    @pl.when(extra_up)
+    def _():
+        pl.semaphore_signal(barrier, inc=1, device_id={"seq": (z + seqs - 1) % seqs, "blk": end},
+                            device_id_type=MESH)
+
+    @pl.when(sends_state)
+    def _():
+        for target in range(1, blks):
+            pl.semaphore_signal(barrier, inc=1, device_id={"seq": below, "blk": target},
+                                device_id_type=MESH)
+
+    pl.semaphore_wait(
+        barrier,
+        has_ahead.astype(jnp.int32) + has_after.astype(jnp.int32)
+        + extra_up.astype(jnp.int32) + end * sends_state.astype(jnp.int32))
 
     @pl.when(has_after)
     def _():
@@ -115,6 +139,11 @@
     col = lax.broadcasted_iota(jnp.int32, (CHUNK, CHUNK), 1)
     head_row = lax.broadcasted_iota(jnp.int32, (heads, CHUNK), 0)
     eye = jnp.where(row == col, 1.0, 0.0)
+
+    @pl.when(x == 0)
+    def _():
+        for head in range(heads):
+            before[head] = jnp.concatenate((eye, jnp.zeros_like(eye)), axis=1).astype(BF16)
 
     def lanes_of(head):
         return pl.ds(pl.multiple_of(head * dim, dim), dim)
@@ -166,10 +195,10 @@
         kv = [jnp.concatenate((k, v), axis=1) for k, v in zip(ks, vs)]
         wu = [r * x.astype(F32) + mm(t * f, x) for r, x, t, f in zip(rates, kv, rest, flat)]
         made = []
-        for k, x in zip(ks, wu):
+        for k, solved in zip(ks, wu):
             turned = k.astype(F32).T.astype(BF16)
             made.append(mm(jnp.concatenate((turned, turned), axis=1),
-                           jnp.concatenate(split(x), axis=0)))
+                           jnp.concatenate(split(solved), axis=0)))
         states = [jnp.concatenate((eye, jnp.zeros((dim, dim), F32)), axis=1)] * PAIR
         for c in range(chunks):
             part = slice(c * CHUNK, (c + 1) * CHUNK)
@@ -188,21 +217,44 @@
             a_ref[pair * PAIR + lane] = jnp.concatenate(split(states[lane][:, :dim]), axis=1)
             b_ref[pair * PAIR + lane] = states[lane][:, dim:]
 
+    def compose(pair):
+        for lane in range(PAIR):
+            head = pair * PAIR + lane
+
+            @pl.when(x > 0)
+            def _():
+                join(head).wait_recv()
+
+            prior = before[head]
+            both = mm(a_ref[head], jnp.concatenate((prior, prior), axis=0))
+            made_map, made_add = both[:, :dim], both[:, dim:] + b_ref[head]
+
+            @pl.when(sends_row)
+            def _():
+                onward[head] = jnp.concatenate((made_map, made_add), axis=1).astype(BF16)
+                join(head).start()
+
+            @pl.when(sends_state)
+            def _():
+                row_a[head] = jnp.concatenate(split(made_map), axis=1)
+                row_b[head] = made_add
+
     def pass_on(pair):
         for lane in range(PAIR):
             head = pair * PAIR + lane
 
-            @pl.when(has_ahead)
+            @pl.when(z > 0)
             def _():
-                move(head).wait_recv()
-
-            @pl.when(has_after)
+                move(head, 0).wait_recv()
+
+            @pl.when(sends_state)
             def _():
                 state = came[head]
                 goes[head] = (
-                    b_ref[head] + mm(a_ref[head], jnp.concatenate((state, state), axis=0))
+                    row_b[head] + mm(row_a[head], jnp.concatenate((state, state), axis=0))
                 ).astype(BF16)
-                move(head).start()
+                for target in range(blks - 1, -1, -1):
+                    move(head, target).start()
 
     def reads_of(pair):
         for lane in range(PAIR):
@@ -219,7 +271,8 @@
     def finish(pair):
         for lane in range(PAIR):
             head = pair * PAIR + lane
-            state = came[head]
+            prior = before[head]
+            state = (mm(prior[:, :dim], came[head]) + prior[:, dim:].astype(F32)).astype(BF16)
             out = known_ref[head] + mm(
                 jnp.concatenate(split(lead_ref[head]), axis=1),
                 jnp.concatenate((state, state), axis=0))
@@ -230,45 +283,66 @@
     def first_part(i, carry):
         maps_of(i)
 
-        @pl.when(i >= here)
-        def _():
-            pass_on(i - here)
+        @pl.when((i >= x) & (i < x + pairs))
+        def _():
+            compose(i - x)
+
+        @pl.when(i >= lag)
+        def _():
+            pass_on(i - lag)
         return carry
 
     def second_part(i, carry):
         reads_of(i - pairs)
 
-        @pl.when((i >= here) & (i < here + pairs))
-        def _():
-            pass_on(i - here)
-
-        @pl.when(here <= pairs)
+        @pl.when((i >= x) & (i < x + pairs))
+        def _():
+            compose(i - x)
+
+        @pl.when((i >= lag) & (i < lag + pairs))
+        def _():
+            pass_on(i - lag)
+
+        @pl.when(lag <= pairs)
         def _():
             finish(i - pairs)
 
-        @pl.when((here > pairs) & (i >= here))
-        def _():
-            finish(i - here)
+        @pl.when((lag > pairs) & (i >= lag))
+        def _():
+            finish(i - lag)
         return carry
 
     def third_part(i, carry):
-        @pl.when(i >= here)
-        def _():
-            pass_on(i - here)
-            finish(i - here)
+        @pl.when((i >= x) & (i < x + pairs))
+        def _():
+            compose(i - x)
+
+        @pl.when(i >= lag)
+        def _():
+            pass_on(i - lag)
+            finish(i - lag)
         return carry
 
     lax.fori_loop(0, pairs, first_part, 0)
     arrive(0)
     lax.fori_loop(pairs, 2 * pairs, second_part, 0)
-    lax.fori_loop(2 * pairs, here + pairs, third_part, 0)
+    lax.fori_loop(2 * pairs, lag + pairs, third_part, 0)
 
     @pl.when(has_after)
     def _():
         for which in range(3):
             rim_move(which).wait_send()
+
+    @pl.when(sends_row)
+    def _():
         for head in range(heads):
-            move(head).wait_send()
+            join(head).wait_send()
+
+    @pl.when(sends_state)
+    def _():
+        for head in range(heads):
+            for target in range(blks):
+                move(head, target).wait_send()
 
 
 def on_device(query_raw, key_raw, value_raw, beta_rate, conv_weight, out_gain):
@@ -298,14 +372,20 @@
             pltpu.VMEM((heads, rows, dim), F32),
             pltpu.VMEM((heads, dim, dim), BF16),
             pltpu.VMEM((heads, dim, dim), BF16),
+            pltpu.VMEM((heads, dim, 2 * dim), BF16),
+            pltpu.VMEM((heads, dim, 2 * dim), BF16),
+            pltpu.VMEM((heads, dim, 2 * dim), BF16),
+            pltpu.VMEM((heads, dim, dim), F32),
             pltpu.SemaphoreType.DMA((3,)),
             pltpu.SemaphoreType.DMA((3,)),
             pltpu.SemaphoreType.DMA((3,)),
             pltpu.SemaphoreType.DMA((heads,)),
             pltpu.SemaphoreType.DMA((heads,)),
+            pltpu.SemaphoreType.DMA((blks, heads)),
+            pltpu.SemaphoreType.DMA((heads,)),
         ],
         compiler_params=pltpu.CompilerParams(
-            collective_id=0, has_side_effects=True, vmem_limit_bytes=56 << 20),
+            collective_id=0, has_side_effects=True, vmem_limit_bytes=52 << 20),
     )(query_raw, key_raw, value_raw, conv_weight, beta_rate.T, out_gain.reshape(1, dim))
 
 

time: 44.7 us -> 39.8 us (0.89)
  the two profiles are of different devices: /device:TPU:26 before, /device:TPU:24 now
where the time goes in v4:
time: 39.8 us; the launch traced here: 39.6 us
  Pallas kernels  36.5 us (92%)
  local copies, waits for them, and re-layouts  3.14 us (8%)
    pallas_call x1, Pallas kernels, on_device(): pl.pallas_call(functools.partial(layer_kernel, seqs, blks, taps), name='l...  36.5 us
    unnamed x7, local copies, waits for them, and re-layouts  3.14 us

profile of v4, /device:TPU:24, one launch (start us, length us, event | category | flops | bytes accessed | tf_op | source)
XLA Modules:
  0.0 39.6 jit_solution(7366455734017163209)
XLA Ops:
  0.0 0.0 copy-start.2
  0.0 0.7 %copy-done.2 = f32[128]{0:T(128)S(1)} copy-done((f32[128]{0:T(128)S(1)}, f32[128]{0:T(128)}, u32[]{:S(2)}) %copy-start.2) | copy-done | bytes 536
  0.7 0.0 copy-start
  0.7 0.8 %copy-done = f32[3,4,1024]{2,1,0:T(4,128)S(1)} copy-done((f32[3,4,1024]{2,1,0:T(4,128)S(1)}, f32[3,4,1024]{2,1,0:T(4,128)}, u32[]{:S(2)}) %copy-start) | copy-done | bytes 49176
  1.5 0.0 copy-start.1
  1.5 0.7 %copy-done.1 = f32[512,8]{0,1:T(8,128)S(1)} copy-done((f32[512,8]{0,1:T(8,128)S(1)}, f32[512,8]{0,1:T(8,128)}, u32[]{:S(2)}) %copy-start.1) | copy-done | bytes 16408
  2.2 36.5 %layer.1 = bf16[512,1024]{1,0:T(8,128)(2,1)S(1)} custom-call(bf16[512,1024]{1,0:T(8,128)(2,1)} %q_hbm.1, bf16[512,1024]{1,0:T(8,128)(2,1)} %k_hbm.1, bf16[512,1024]{1,0:T(8,128)(2,1)} %v_hbm.1, f32[3,4,1024]{2,1,0:T(4,128)S(1)} %copy-done, f32[8,512]{1,0:T(8,128)S(1)} %bitcast.2, f32[1,128]{1,0:T(1,128)S(1)} %bitcast.3), custom_call_target="tpu_custom_call" | custom-call | tf_op jit(solution)/shard_map/layer/pallas_call | solution.py:356
  38.6 1.0 %copy.8 = bf16[512,1024]{1,0:T(8,128)(2,1)} copy(bf16[512,1024]{1,0:T(8,128)(2,1)S(1)} %layer.1) | data formatting | bytes 2097152
Async XLA Ops:
  0.0 0.7 %copy-start.2 = (f32[128]{0:T(128)S(1)}, f32[128]{0:T(128)}, u32[]{:S(2)}) copy-start(f32[128]{0:T(128)} %param.11) | copy-start | bytes 1540
  0.7 0.8 %copy-start = (f32[3,4,1024]{2,1,0:T(4,128)S(1)}, f32[3,4,1024]{2,1,0:T(4,128)}, u32[]{:S(2)}) copy-start(f32[3,4,1024]{2,1,0:T(4,128)} %w_ref.1) | copy-start | bytes 147460
  1.5 0.7 %copy-start.1 = (f32[512,8]{0,1:T(8,128)S(1)}, f32[512,8]{0,1:T(8,128)}, u32[]{:S(2)}) copy-start(f32[512,8]{0,1:T(8,128)} %param.9) | copy-start | bytes 49156

commit v5 on v4

--- a/solution.py
+++ b/solution.py
@@ -13,7 +13,7 @@
 RIM = 16
 LEAD = 8
 PAIR = 2
-SMALL = 16
+SMALL = 8
 MESH = pl.DeviceIdType.MESH
 
 
@@ -187,10 +187,25 @@
         rest = [x + y + mm(x, y) for x, y in zip(rest, power)]
         size = SMALL
         while size < CHUNK:
-            band = (row // (2 * size) == col // (2 * size)) & (row // size != col // size)
-            off = [jnp.where(band, x, 0.0) for x in lower]
+            cuts = range(0, CHUNK, size)
+
+            def odd(x):
+                return jnp.concatenate([x[n:n + size] for n in cuts[1::2]], axis=0)
+
+            def joined(evens, odds):
+                rows_of = []
+                for n, start in enumerate(cuts[0::2]):
+                    rows_of.append(evens[start:start + size])
+                    rows_of.append(odds[n * size:(n + 1) * size])
+                return jnp.concatenate(rows_of, axis=0)
+
+            band = odd(row // size) == odd(col // size) + 1
+            blank = jnp.zeros((CHUNK, CHUNK), F32)
+            off = [jnp.where(band, odd(x), 0.0) for x in lower]
             mid = [x + mm(x, y) for x, y in zip(off, rest)]
-            rest = [x - y - mm(x, y) for x, y in zip(rest, mid)]
+            rest = [
+                joined(x, odd(x) - y - mm(odd(x), joined(blank, y))) for x, y in zip(rest, mid)
+            ]
             size *= 2
         kv = [jnp.concatenate((k, v), axis=1) for k, v in zip(ks, vs)]
         wu = [r * x.astype(F32) + mm(t * f, x) for r, x, t, f in zip(rates, kv, rest, flat)]

time: 39.8 us -> 40 us (level)
  no operation moved by 1% of the time
where the time goes in v5:
time: 40 us; the launch traced here: 39.7 us
  Pallas kernels  36.6 us (92%)
  local copies, waits for them, and re-layouts  3.14 us (8%)
    pallas_call x1, Pallas kernels, on_device(): pl.pallas_call(functools.partial(layer_kernel, seqs, blks, taps), name='l...  36.6 us
    unnamed x7, local copies, waits for them, and re-layouts  3.14 us

profile of v5, /device:TPU:24, one launch (start us, length us, event | category | flops | bytes accessed | tf_op | source)
XLA Modules:
  0.0 39.7 jit_solution(7086927017491468265)
XLA Ops:
  0.0 0.0 copy-start.2
  0.0 0.7 %copy-done.2 = f32[128]{0:T(128)S(1)} copy-done((f32[128]{0:T(128)S(1)}, f32[128]{0:T(128)}, u32[]{:S(2)}) %copy-start.2) | copy-done | bytes 536
  0.7 0.0 copy-start
  0.7 0.8 %copy-done = f32[3,4,1024]{2,1,0:T(4,128)S(1)} copy-done((f32[3,4,1024]{2,1,0:T(4,128)S(1)}, f32[3,4,1024]{2,1,0:T(4,128)}, u32[]{:S(2)}) %copy-start) | copy-done | bytes 49176
  1.5 0.0 copy-start.1
  1.5 0.7 %copy-done.1 = f32[512,8]{0,1:T(8,128)S(1)} copy-done((f32[512,8]{0,1:T(8,128)S(1)}, f32[512,8]{0,1:T(8,128)}, u32[]{:S(2)}) %copy-start.1) | copy-done | bytes 16408
  2.2 36.6 %layer.1 = bf16[512,1024]{1,0:T(8,128)(2,1)S(1)} custom-call(bf16[512,1024]{1,0:T(8,128)(2,1)} %q_hbm.1, bf16[512,1024]{1,0:T(8,128)(2,1)} %k_hbm.1, bf16[512,1024]{1,0:T(8,128)(2,1)} %v_hbm.1, f32[3,4,1024]{2,1,0:T(4,128)S(1)} %copy-done, f32[8,512]{1,0:T(8,128)S(1)} %bitcast.2, f32[1,128]{1,0:T(1,128)S(1)} %bitcast.3), custom_call_target="tpu_custom_call" | custom-call | tf_op jit(solution)/shard_map/layer/pallas_call | solution.py:371
  38.8 1.0 %copy.8 = bf16[512,1024]{1,0:T(8,128)(2,1)} copy(bf16[512,1024]{1,0:T(8,128)(2,1)S(1)} %layer.1) | data formatting | bytes 2097152
Async XLA Ops:
  0.0 0.7 %copy-start.2 = (f32[128]{0:T(128)S(1)}, f32[128]{0:T(128)}, u32[]{:S(2)}) copy-start(f32[128]{0:T(128)} %param.11) | copy-start | bytes 1540
  0.7 0.8 %copy-start = (f32[3,4,1024]{2,1,0:T(4,128)S(1)}, f32[3,4,1024]{2,1,0:T(4,128)}, u32[]{:S(2)}) copy-start(f32[3,4,1024]{2,1,0:T(4,128)} %w_ref.1) | copy-start | bytes 147460
  1.5 0.7 %copy-start.1 = (f32[512,8]{0,1:T(8,128)S(1)}, f32[512,8]{0,1:T(8,128)}, u32[]{:S(2)}) copy-start(f32[512,8]{0,1:T(8,128)} %param.9) | copy-start | bytes 49156

commit v6 on v4

--- a/solution.py
+++ b/solution.py
@@ -253,8 +253,13 @@
                 goes[head] = (
                     row_b[head] + mm(row_a[head], jnp.concatenate((state, state), axis=0))
                 ).astype(BF16)
-                for target in range(blks - 1, -1, -1):
-                    move(head, target).start()
+                move(head, blks - 1).start()
+
+        @pl.when(sends_state)
+        def _():
+            for lane in range(PAIR):
+                for target in range(blks - 1):
+                    move(pair * PAIR + lane, target).start()
 
     def reads_of(pair):
         for lane in range(PAIR):

time: 39.8 us -> 38.6 us (0.970)
  Pallas kernels: 36.5 us -> 35.2 us
    pallas_call x1, Pallas kernels: 36.5 us -> 35.2 us  [on_device(): pl.pallas_call(functools.partial(layer_kernel, seqs, blks, taps), name='l...]
where the time goes in v6:
time: 38.6 us; the launch traced here: 38.4 us
  Pallas kernels  35.2 us (91%)
  local copies, waits for them, and re-layouts  3.14 us (8%)
    pallas_call x1, Pallas kernels, on_device(): pl.pallas_call(functools.partial(layer_kernel, seqs, blks, taps), name='l...  35.2 us
    unnamed x7, local copies, waits for them, and re-layouts  3.14 us

profile of v6, /device:TPU:24, one launch (start us, length us, event | category | flops | bytes accessed | tf_op | source)
XLA Modules:
  0.0 38.4 jit_solution(8870320982594870505)
XLA Ops:
  0.0 0.0 copy-start.2
  0.0 0.7 %copy-done.2 = f32[128]{0:T(128)S(1)} copy-done((f32[128]{0:T(128)S(1)}, f32[128]{0:T(128)}, u32[]{:S(2)}) %copy-start.2) | copy-done | bytes 536
  0.7 0.0 copy-start
  0.7 0.8 %copy-done = f32[3,4,1024]{2,1,0:T(4,128)S(1)} copy-done((f32[3,4,1024]{2,1,0:T(4,128)S(1)}, f32[3,4,1024]{2,1,0:T(4,128)}, u32[]{:S(2)}) %copy-start) | copy-done | bytes 49176
  1.5 0.0 copy-start.1
  1.5 0.7 %copy-done.1 = f32[512,8]{0,1:T(8,128)S(1)} copy-done((f32[512,8]{0,1:T(8,128)S(1)}, f32[512,8]{0,1:T(8,128)}, u32[]{:S(2)}) %copy-start.1) | copy-done | bytes 16408
  2.2 35.2 %layer.1 = bf16[512,1024]{1,0:T(8,128)(2,1)S(1)} custom-call(bf16[512,1024]{1,0:T(8,128)(2,1)} %q_hbm.1, bf16[512,1024]{1,0:T(8,128)(2,1)} %k_hbm.1, bf16[512,1024]{1,0:T(8,128)(2,1)} %v_hbm.1, f32[3,4,1024]{2,1,0:T(4,128)S(1)} %copy-done, f32[8,512]{1,0:T(8,128)S(1)} %bitcast.2, f32[1,128]{1,0:T(1,128)S(1)} %bitcast.3), custom_call_target="tpu_custom_call" | custom-call | tf_op jit(solution)/shard_map/layer/pallas_call | solution.py:361
  37.4 1.0 %copy.8 = bf16[512,1024]{1,0:T(8,128)(2,1)} copy(bf16[512,1024]{1,0:T(8,128)(2,1)S(1)} %layer.1) | data formatting | bytes 2097152
Async XLA Ops:
  0.0 0.7 %copy-start.2 = (f32[128]{0:T(128)S(1)}, f32[128]{0:T(128)}, u32[]{:S(2)}) copy-start(f32[128]{0:T(128)} %param.11) | copy-start | bytes 1540
  0.7 0.8 %copy-start = (f32[3,4,1024]{2,1,0:T(4,128)S(1)}, f32[3,4,1024]{2,1,0:T(4,128)}, u32[]{:S(2)}) copy-start(f32[3,4,1024]{2,1,0:T(4,128)} %w_ref.1) | copy-start | bytes 147460
  1.5 0.7 %copy-start.1 = (f32[512,8]{0,1:T(8,128)S(1)}, f32[512,8]{0,1:T(8,128)}, u32[]{:S(2)}) copy-start(f32[512,8]{0,1:T(8,128)} %param.9) | copy-start | bytes 49156
